TPU v7x, 512 devices: a whole 4x4x16 slice. The times are simulated.
512 devices in a mesh: grid: 4 (over z_lo), gx: 16 (over x, y), gy: 8 (over z_hi, core).
Axes of the slice: x: 4, y: 4, z: 16 (z_hi: 4, z_lo: 4; z = z_hi * 4 + z_lo), core: 2. Of those that a mesh axis runs over, the one named last changes fastest.
Arguments:
- adjoint: float32 [4, 24, 512, 2048], P('grid', None, 'gx', 'gy'), may hold values from -6 to 6
- sea_mask: int32 [4, 512, 2048], P('grid', 'gx', 'gy'), may hold values 0 or 1
- diffusivity: float32 [4, 512, 2048], P('grid', 'gx', 'gy'), may hold values from 0.03 to 0.24
- aggregation: float32 [4, 512, 2048], P('grid', 'gx', 'gy'), may hold values from 0.02 to 0.3
- breakup: float32 [4, 512, 2048], P('grid', 'gx', 'gy'), may hold values from 0.02 to 0.3
- sponge: float32 [4, 512, 2048], P('grid', 'gx', 'gy'), may hold values from 0.05 to 0.6
- settling: float32 [4, 3], replicated, may hold values from 0.05 to 0.5
- partner_flip: int32 [3, 16, 8], replicated, may hold values from 0 to 1
- row_offset: int32 [3, 16, 8], replicated, may hold values from 0 to 16
- col_offset: int32 [3, 16, 8], replicated, may hold values from 0 to 128
Outputs:
- adjoint_out: float32 [4, 24, 512, 2048], P('grid', None, 'gx', 'gy')
Inputs may be any that keep to these rules, and one draw needn't show every extreme that they name: `partner_flip`: every child tile is paired with exactly one parent tile in its own tile column, in its own tile row or the row whose index differs in the lowest bit; a parent tile serves 0 to 6 child tiles. `row_offset`: the footprint lies inside the paired parent tile. `col_offset`: the footprint lies inside the paired parent tile.
All inputs are finite; a program needn't handle non-finite values. No bound on the sum of `sea_mask` on one device may be relied on, other than what follows from the above.
Results may differ from a plain program's by a relative error of at most 0.0001.
Values sent between devices are 32-bit elements; how exact they have to be, the bound alone decides.
A program may use at most 64 MiB of HBM per device.

v0:
```python
import jax
import jax.numpy as jnp
from jax import lax
from jax.sharding import PartitionSpec as P

NCLS = 3
LEV = 8
STEPS = 2


relaxation = 0.125


def partner(value, axis, distance):
    mask = 2**distance
    pairs = [(source, source ^ mask) for source in range(lax.axis_size(axis))]
    return lax.ppermute(value, axis, pairs)


def spread(block, axis, holder):
    block = jnp.where(lax.axis_index(axis) == holder, block, jnp.zeros_like(block))
    return lax.psum(block, axis)


def padded_2(shard, sides, width):
    for axis, dim in sides:
        size, length = (lax.axis_size(axis), shard.shape[dim])
        up = [(i, (i + 1) % size) for i in range(size - 1)]
        down = [(j, i) for i, j in up]
        last = lax.slice_in_dim(shard, length - width, length, axis=dim)
        leading = lax.slice_in_dim(shard, 0, width, axis=dim)
        before = lax.ppermute(last, axis, up)
        after = lax.ppermute(leading, axis, down)
        shard = jnp.concatenate([before, shard, after], axis=dim)
    return shard


def block_sums(values):
    shape = values.shape
    return values.reshape(shape[:-2] + (shape[-2] // 2, 2, shape[-1] // 2, 2)).sum(axis=(-3, -1))


def expand_cells(values):
    return jnp.repeat(jnp.repeat(values, 2, axis=-2), 2, axis=-1)


def floc_adjoint(values, aggregation, breakup):
    shape = values.shape
    split = values.reshape((shape[0], NCLS, LEV) + shape[2:])
    agg = aggregation[:, None]
    brk = breakup[:, None]
    first = split[:, 0]
    second = split[:, 1]
    third = split[:, 2]
    new_first = (1.0 - agg) * first + agg * second
    new_second = brk * first + (1.0 - agg - brk) * second + agg * third
    new_third = brk * second + (1.0 - brk) * third
    return jnp.stack([new_first, new_second, new_third], axis=1).reshape(shape)


def settle_adjoint(values, rates):
    shape = values.shape
    split = values.reshape((shape[0], NCLS, LEV) + shape[2:])
    below = jnp.concatenate([split[:, :, 1:], jnp.zeros_like(split[:, :, :1])], axis=2)
    speed = rates[:, :, None, None, None]
    return ((1.0 - speed) * split + speed * below).reshape(shape)


def local(
    adjoint,
    sea_mask,
    diffusivity,
    aggregation,
    breakup,
    sponge,
    settling,
    partner_flip,
    row_offset,
    col_offset,
):
    n_grid = lax.axis_size("grid")
    slots = n_grid - 1
    grid_index = lax.axis_index("grid")
    row_index = lax.axis_index("gx")
    col_index = lax.axis_index("gy")
    partner_row = jnp.bitwise_xor(row_index, 1)
    is_parent = grid_index == 0
    own_slot = jnp.maximum(grid_index - 1, 0)
    flips_here = partner_flip[:, row_index, col_index]
    flips_there = partner_flip[:, partner_row, col_index]
    tops_here = row_offset[:, row_index, col_index]
    lefts_here = col_offset[:, row_index, col_index]
    tops_there = row_offset[:, partner_row, col_index]
    lefts_there = col_offset[:, partner_row, col_index]
    keep_here = (flips_here == 0).astype(jnp.float32)
    take_there = (flips_there == 1).astype(jnp.float32)
    components = adjoint.shape[1]
    cells_r = adjoint.shape[2]
    cells_c = adjoint.shape[3]
    half_r = cells_r // 2
    half_c = cells_c // 2
    anchor = jnp.zeros((), jnp.int32)
    settle_rates = settling[grid_index][None]
    weights = sponge[0]
    wet_mask = sea_mask.astype(jnp.float32)[:, None]
    row_ids = lax.broadcasted_iota(jnp.int32, (cells_r, cells_c), 0)
    col_ids = lax.broadcasted_iota(jnp.int32, (cells_r, cells_c), 1)
    covered = jnp.zeros((cells_r, cells_c), jnp.float32)
    for slot in range(slots):
        for tops, lefts, flags in (
            (tops_here, lefts_here, keep_here),
            (tops_there, lefts_there, take_there),
        ):
            inside = (
                (row_ids >= tops[slot])
                & (row_ids < tops[slot] + half_r)
                & (col_ids >= lefts[slot])
                & (col_ids < lefts[slot] + half_c)
            )
            covered = covered + flags[slot] * inside.astype(jnp.float32)
    state = adjoint
    for step_number in range(STEPS):
        current = state[0]
        child_block = block_sums(weights * current)
        down_here = jnp.stack(
            [
                keep_here[slot]
                * lax.dynamic_slice(
                    current,
                    (anchor, tops_here[slot], lefts_here[slot]),
                    (components, half_r, half_c),
                )
                for slot in range(slots)
            ]
        )
        down_there = jnp.stack(
            [
                take_there[slot]
                * lax.dynamic_slice(
                    current,
                    (anchor, tops_there[slot], lefts_there[slot]),
                    (components, half_r, half_c),
                )
                for slot in range(slots)
            ]
        )
        gathered_up = lax.all_gather(child_block[None], "grid", axis=0, tiled=True)[1:]
        up_keep = keep_here[:, None, None, None] * gathered_up
        up_send = (1.0 - keep_here)[:, None, None, None] * gathered_up
        up_cross, down_cross = partner((up_send, down_there), "gx", 0)
        down_all = spread(down_here + down_cross, "grid", 0)
        from_parent = down_all[own_slot]
        child_new = (1.0 - weights) * current + relaxation / 4.0 * expand_cells(from_parent)
        gathered = jnp.zeros_like(current)
        for slot in range(slots):
            for tops, lefts, pieces in (
                (tops_here, lefts_here, up_keep),
                (tops_there, lefts_there, up_cross),
            ):
                existing = lax.dynamic_slice(
                    gathered, (anchor, tops[slot], lefts[slot]), (components, half_r, half_c)
                )
                gathered = lax.dynamic_update_slice(
                    gathered, existing + pieces[slot], (anchor, tops[slot], lefts[slot])
                )
        parent_new = (1.0 - relaxation * covered) * current + gathered
        state = jnp.where(is_parent, parent_new, child_new)[None]
        state = floc_adjoint(state, aggregation, breakup)
        state = settle_adjoint(state, settle_rates)
        wet = wet_mask * state
        flux = diffusivity[:, None] * wet
        padded = padded_2(flux, (("gx", 2), ("gy", 3)), 1)
        state = (
            wet
            + padded[:, :, :-2, 1:-1]
            + padded[:, :, 2:, 1:-1]
            + padded[:, :, 1:-1, :-2]
            + padded[:, :, 1:-1, 2:]
            - 4.0 * flux
        )
    return state


def solution(mesh):
    in_specs = (
        P("grid", None, "gx", "gy"),
        P("grid", "gx", "gy"),
        P("grid", "gx", "gy"),
        P("grid", "gx", "gy"),
        P("grid", "gx", "gy"),
        P("grid", "gx", "gy"),
        P(),
        P(),
        P(),
        P(),
    )
    out_specs = P("grid", None, "gx", "gy")
    return jax.shard_map(local, mesh=mesh, in_specs=in_specs, out_specs=out_specs, check_vma=False)
```

profile of v0, /device:TPU:1, one launch (start us, length us, event | category | flops | bytes accessed | tf_op | source)
XLA Modules:
  0.0 420.3 jit_solution(10322343063372970234)
XLA Ops:
  33.4 7.3 %dynamic-slice_multiply_fusion.11 = (f32[1,24,16,128]{3,2,1,0:T(8,128)}, f32[1,24,16,128]{3,2,1,0:T(8,128)S(1)}, f32[1,24,16,128]{3,2,1,0:T(8,128)}, f32[1,24,16...) fusion(f32[1,24,32,256]{3,2,1,0:T(8,128)} %param.10, s32[]{:T(128)S(6)} %select_n.61, ...), kind=kLoop, calls=%fused_computation.97 | loop fusion | flops 294912 | bytes 2359368 | tf_op jit(solution)/shard_map/mul | solution.py:127
  50.4 7.2 %multiply_reduce_fusion.1 = f32[24,16,128]{0,2,1:T(8,128)} fusion(f32[24,16,2,128,2]{0,4,3,2,1:T(2,128)} %bitcast.116, f32[16,2,128,2]{3,2,1,0:T(8,128)S(1)} %mul.540), kind=kLoop, calls=%fused_computation.1 | loop fusion | flops 344064 | bytes 1015808 | tf_op jit(solution)/shard_map/reduce_sum | solution.py:40
  59.1 18.5 %all-gather = f32[96,16,128]{2,1,0:T(8,128)S(1)} all-gather(f32[24,16,128]{2,1,0:T(8,128)S(1)} %copy.39), channel_id=2, replica_groups=mesh['grid'=4,'gx'=16,'gy'=8] {'grid'}, dimensions={0}, use_global_device_ids=true | all-gather | bytes 983040 | tf_op jit(solution)/shard_map/all_gather | solution.py:147
  101.9 9.0 %dynamic_update_slice.36 = f32[24,32,256]{2,1,0:T(8,128)} dynamic-update-slice(f32[24,32,256]{2,1,0:T(8,128)} %broadcast.563.clone, f32[24,16,128]{2,1,0:T(8,128)} %slice_bitcast_fusion.11, s32[]{:T(128)} %constant.55.clone.1, s32[]{:T(128)S(6)} %select_n.61, s32[]{:T(128)S(6)} %select_n.62) | dynamic-update-slice | bytes 393220 | tf_op jit(solution)/shard_map/dynamic_update_slice | solution.py:163
  118.0 9.0 %dynamic_update_slice.37 = f32[24,32,256]{2,1,0:T(8,128)} dynamic-update-slice(f32[24,32,256]{2,1,0:T(8,128)} %dynamic_update_slice.36, f32[24,16,128]{2,1,0:T(8,128)} %fusion.27, s32[]{:T(128)} %constant.55.clone.1, s32[]{:T(128)S(6)} %select_n.63, s32[]{:T(128)S(6)} %select_n.64) | dynamic-update-slice | bytes 393220 | tf_op jit(solution)/shard_map/dynamic_update_slice | solution.py:163
  128.8 9.0 %dynamic_update_slice.38 = f32[24,32,256]{2,1,0:T(8,128)} dynamic-update-slice(f32[24,32,256]{2,1,0:T(8,128)} %dynamic_update_slice.37, f32[24,16,128]{2,1,0:T(8,128)} %fusion.26, s32[]{:T(128)} %constant.55.clone.1, s32[]{:T(128)S(6)} %select_n.65, s32[]{:T(128)S(6)} %select_n.66) | dynamic-update-slice | bytes 393220 | tf_op jit(solution)/shard_map/dynamic_update_slice | solution.py:163
  139.7 8.4 %dynamic_update_slice.39 = f32[24,32,256]{2,1,0:T(8,128)} dynamic-update-slice(f32[24,32,256]{2,1,0:T(8,128)} %dynamic_update_slice.38, f32[24,16,128]{2,1,0:T(8,128)} %fusion.25, s32[]{:T(128)} %constant.55.clone.1, s32[]{:T(128)S(6)} %select_n.67, s32[]{:T(128)S(6)} %select_n.68) | dynamic-update-slice | bytes 393220 | tf_op jit(solution)/shard_map/dynamic_update_slice | solution.py:163
  150.0 9.0 %dynamic_update_slice.40 = f32[24,32,256]{2,1,0:T(8,128)} dynamic-update-slice(f32[24,32,256]{2,1,0:T(8,128)} %dynamic_update_slice.39, f32[24,16,128]{2,1,0:T(8,128)} %fusion.24, s32[]{:T(128)} %constant.55.clone.1, s32[]{:T(128)S(6)} %select_n.69, s32[]{:T(128)S(6)} %select_n.70) | dynamic-update-slice | bytes 393220 | tf_op jit(solution)/shard_map/dynamic_update_slice | solution.py:163
  160.3 9.0 %dynamic_update_slice.41 = f32[24,32,256]{2,1,0:T(8,128)} dynamic-update-slice(f32[24,32,256]{2,1,0:T(8,128)} %dynamic_update_slice.40, f32[24,16,128]{2,1,0:T(8,128)S(1)} %fusion.23, s32[]{:T(128)} %constant.55.clone.1, s32[]{:T(128)S(6)} %select_n.71, s32[]{:T(128)S(6)} %select_n.72) | dynamic-update-slice | bytes 393220 | tf_op jit(solution)/shard_map/dynamic_update_slice | solution.py:163
  169.3 13.2 %all-reduce.5.cloned.1.call-done = f32[3,24,16,128]{3,2,1,0:T(8,128)} async-done(((f32[3,24,16,128]{3,2,1,0:T(8,128)}), f32[3,24,16,128]{3,2,1,0:T(8,128)}) %all-reduce.5.cloned.1.call-update) | async-done | bytes 589840 | tf_op jit(solution)/shard_map/psum | solution.py:22
  202.0 11.7 %collective-permute-start.4 = (f32[1,24,34,1]{3,2,1,0:T(8,128)S(1)}, f32[1,24,34,1]{3,2,1,0:T(8,128)S(1)}, u32[]{:S(2)}, u32[]{:S(2)}) collective-permute-start(f32[1,24,34,1]{3,2,1,0:T(8,128)S(1)} %get-tuple-element.11), channel_id=1, source_target_pairs={{0,1},{1,2},{2,3},{3,4},{4,5},{5,6},{6,7},{8,9},{9,10},{10,11},{11... | collective-permute-start | bytes 9800 | tf_op jit(solution)/shard_map/ppermute | solution.py:32
  219.6 23.1 %collective-permute-done.5 = f32[1,24,34,1]{3,2,1,0:T(8,128)S(1)} collective-permute-done((f32[1,24,34,1]{3,2,1,0:T(8,128)S(1)}, f32[1,24,34,1]{3,2,1,0:T(8,128)S(1)}, u32[]{:S(2)}, u32[]{:S(2)}) %collective-permute-start.5) | collective-permute-done | bytes 3296 | tf_op jit(solution)/shard_map/ppermute | solution.py:33
  243.5 5.0 %dynamic-slice_multiply_fusion.5 = (f32[1,24,16,128]{3,2,1,0:T(8,128)}, f32[1,24,16,128]{3,2,1,0:T(8,128)S(1)}, f32[1,24,16,128]{3,2,1,0:T(8,128)S(1)}, f32[1,24...) fusion(f32[1,24,32,256]{3,2,1,0:T(8,128)S(1)} %fusion.6, s32[]{:T(128)S(6)} %select_n.61, ...), kind=kLoop, calls=%fused_computation.90 | loop fusion | flops 294912 | bytes 2359368 | tf_op jit(solution)/shard_map/mul | solution.py:127
  255.2 7.2 %multiply_reduce_fusion = f32[24,16,128]{0,2,1:T(8,128)} fusion(f32[24,16,2,128,2]{0,4,3,2,1:T(2,128)} %bitcast.115, f32[16,2,128,2]{3,2,1,0:T(8,128)S(1)} %mul.540), kind=kLoop, calls=%fused_computation | loop fusion | flops 344064 | bytes 1015808 | tf_op jit(solution)/shard_map/reduce_sum | solution.py:40
  264.0 12.8 %all-gather.1 = f32[96,16,128]{2,1,0:T(8,128)S(1)} all-gather(f32[24,16,128]{2,1,0:T(8,128)S(1)} %copy.44), channel_id=3, replica_groups=mesh['grid'=4,'gx'=16,'gy'=8] {'grid'}, dimensions={0}, use_global_device_ids=true | all-gather | bytes 983040 | tf_op jit(solution)/shard_map/all_gather | solution.py:147
  280.0 7.9 %dynamic_update_slice.42 = f32[24,32,256]{2,1,0:T(8,128)S(1)} dynamic-update-slice(f32[24,32,256]{2,1,0:T(8,128)S(1)} %broadcast.563, f32[24,16,128]{2,1,0:T(8,128)S(1)} %slice_bitcast_fusion.5, s32[]{:T(128)} %constant.55.clone.1, s32[]{:T(128)S(6)} %select_n.61, s32[]{:T(128)S(6)} %select_n.62) | dynamic-update-slice | bytes 393220 | tf_op jit(solution)/shard_map/dynamic_update_slice | solution.py:163
  290.0 7.9 %dynamic_update_slice.43 = f32[24,32,256]{2,1,0:T(8,128)S(1)} dynamic-update-slice(f32[24,32,256]{2,1,0:T(8,128)S(1)} %dynamic_update_slice.42, f32[24,16,128]{2,1,0:T(8,128)S(1)} %fusion.22, s32[]{:T(128)} %constant.55.clone.1, s32[]{:T(128)S(6)} %select_n.63, s32[]{:T(128)S(6)} %select_n.64) | dynamic-update-slice | bytes 393220 | tf_op jit(solution)/shard_map/dynamic_update_slice | solution.py:163
  298.1 7.9 %dynamic_update_slice.44 = f32[24,32,256]{2,1,0:T(8,128)S(1)} dynamic-update-slice(f32[24,32,256]{2,1,0:T(8,128)S(1)} %dynamic_update_slice.43, f32[24,16,128]{2,1,0:T(8,128)S(1)} %fusion.21, s32[]{:T(128)} %constant.55.clone.1, s32[]{:T(128)S(6)} %select_n.65, s32[]{:T(128)S(6)} %select_n.66) | dynamic-update-slice | bytes 393220 | tf_op jit(solution)/shard_map/dynamic_update_slice | solution.py:163
  306.1 7.7 %dynamic_update_slice.45 = f32[24,32,256]{2,1,0:T(8,128)S(1)} dynamic-update-slice(f32[24,32,256]{2,1,0:T(8,128)S(1)} %dynamic_update_slice.44, f32[24,16,128]{2,1,0:T(8,128)S(1)} %fusion.20, s32[]{:T(128)} %constant.55.clone.1, s32[]{:T(128)S(6)} %select_n.67, s32[]{:T(128)S(6)} %select_n.68) | dynamic-update-slice | bytes 393220 | tf_op jit(solution)/shard_map/dynamic_update_slice | solution.py:163
  314.0 7.9 %dynamic_update_slice.46 = f32[24,32,256]{2,1,0:T(8,128)S(1)} dynamic-update-slice(f32[24,32,256]{2,1,0:T(8,128)S(1)} %dynamic_update_slice.45, f32[24,16,128]{2,1,0:T(8,128)S(1)} %fusion.19, s32[]{:T(128)} %constant.55.clone.1, s32[]{:T(128)S(6)} %select_n.69, s32[]{:T(128)S(6)} %select_n.70) | dynamic-update-slice | bytes 393220 | tf_op jit(solution)/shard_map/dynamic_update_slice | solution.py:163
  322.1 7.9 %dynamic_update_slice.47 = f32[24,32,256]{2,1,0:T(8,128)S(1)} dynamic-update-slice(f32[24,32,256]{2,1,0:T(8,128)S(1)} %dynamic_update_slice.46, f32[24,16,128]{2,1,0:T(8,128)S(1)} %fusion.18, s32[]{:T(128)} %constant.55.clone.1, s32[]{:T(128)S(6)} %select_n.71, s32[]{:T(128)S(6)} %select_n.72) | dynamic-update-slice | bytes 393220 | tf_op jit(solution)/shard_map/dynamic_update_slice | solution.py:163
  330.0 22.0 %all-reduce.7.cloned.1.call-done = f32[3,24,16,128]{3,2,1,0:T(8,128)} async-done(((f32[3,24,16,128]{3,2,1,0:T(8,128)}), f32[3,24,16,128]{3,2,1,0:T(8,128)}) %all-reduce.7.cloned.1.call-update) | async-done | bytes 589840 | tf_op jit(solution)/shard_map/psum | solution.py:22
  371.4 11.7 %collective-permute-start.10 = (f32[1,24,34,1]{3,2,1,0:T(8,128)S(1)}, f32[1,24,34,1]{3,2,1,0:T(8,128)S(1)}, u32[]{:S(2)}, u32[]{:S(2)}) collective-permute-start(f32[1,24,34,1]{3,2,1,0:T(8,128)S(1)} %get-tuple-element.9), channel_id=1, source_target_pairs={{0,1},{1,2},{2,3},{3,4},{4,5},{5,6},{6,7},{8,9},{9,10},{10,11},{11... | collective-permute-start | bytes 9800 | tf_op jit(solution)/shard_map/ppermute | solution.py:32
  389.0 22.8 %collective-permute-done.11 = f32[1,24,34,1]{3,2,1,0:T(8,128)S(1)} collective-permute-done((f32[1,24,34,1]{3,2,1,0:T(8,128)S(1)}, f32[1,24,34,1]{3,2,1,0:T(8,128)S(1)}, u32[]{:S(2)}, u32[]{:S(2)}) %collective-permute-start.11) | collective-permute-done | bytes 3296 | tf_op jit(solution)/shard_map/ppermute | solution.py:33
  (148 shorter events, 113.4 us)
Async XLA Ops:
  6.5 39.1 %copy-start = (f32[1,24,32,256]{3,2,1,0:T(8,128)S(1)}, f32[1,24,32,256]{3,2,1,0:T(8,128)}, u32[]{:S(2)}) copy-start(f32[1,24,32,256]{3,2,1,0:T(8,128)} %param.10) | copy-start | bytes 2359300
  6.5 176.0 %all-reduce.5.cloned.1.call-start = ((), (), s32[]{:S(2)}) async-start(), calls=%async_computation | async-start | bytes 1179648 | tf_op jit(solution)/shard_map/psum | solution.py:22
  33.4 14.9 %copy-start.15 = (f32[1,32,256]{2,1,0:T(8,128)S(1)}, f32[1,32,256]{2,1,0:T(8,128)}, u32[]{:S(2)}) copy-start(f32[1,32,256]{2,1,0:T(8,128)} %param.15) | copy-start | bytes 98308
  41.6 72.2 %collective-permute-start.1 = (f32[3,24,16,128]{3,2,1,0:T(8,128)}, f32[3,24,16,128]{3,2,1,0:T(8,128)}, u32[]{:S(2)}, u32[]{:S(2)}) collective-permute-start(f32[3,24,16,128]{3,2,1,0:T(8,128)} %pad_maximum_fusion.20), channel_id=1, source_target_pairs={{0,8},{8,0},{16,24},{24,16},{32,40},{40,32},{48,56},{56,48},{64,72... | collective-permute-start | bytes 1769480 | tf_op jit(solution)/shard_map/ppermute | solution.py:17
  78.6 37.3 %collective-permute-start = (f32[3,24,16,128]{3,2,1,0:T(8,128)}, f32[3,24,16,128]{3,2,1,0:T(8,128)}, u32[]{:S(2)}, u32[]{:S(2)}) collective-permute-start(f32[3,24,16,128]{3,2,1,0:T(8,128)} %get-tuple-element.37), channel_id=1, source_target_pairs={{0,8},{8,0},{16,24},{24,16},{32,40},{40,32},{48,56},{56,48},{64,72... | collective-permute-start | bytes 1769480 | tf_op jit(solution)/shard_map/ppermute | solution.py:17
  115.9 236.1 %all-reduce.7.cloned.1.call-start = ((), (), s32[]{:S(2)}) async-start(), calls=%async_computation.1 | async-start | bytes 1179648 | tf_op jit(solution)/shard_map/psum | solution.py:22
  185.2 6.4 %copy-start.3 = (f32[32,256]{1,0:T(8,128)S(1)}, f32[32,256]{1,0:T(8,128)}, u32[]{:S(2)}) copy-start(f32[32,256]{1,0:T(8,128)} %multiply_subtract_fusion) | copy-start | bytes 98308
  188.5 4.8 %copy-start.7 = (f32[1,32,256]{2,1,0:T(8,128)S(1)}, f32[1,32,256]{2,1,0:T(8,128)}, u32[]{:S(2)}) copy-start(f32[1,32,256]{2,1,0:T(8,128)} %param.14) | copy-start | bytes 98308
  188.5 4.8 %copy-start.9 = (f32[32,256]{1,0:T(8,128)S(1)}, f32[32,256]{1,0:T(8,128)}, u32[]{:S(2)}) copy-start(f32[32,256]{1,0:T(8,128)} %get-tuple-element.39) | copy-start | bytes 98308
  188.5 4.8 %copy-start.11 = (f32[32,256]{1,0:T(8,128)S(1)}, f32[32,256]{1,0:T(8,128)}, u32[]{:S(2)}) copy-start(f32[32,256]{1,0:T(8,128)} %get-tuple-element.40) | copy-start | bytes 98308
  188.5 4.8 %copy-start.13 = (f32[32,256]{1,0:T(8,128)S(1)}, f32[32,256]{1,0:T(8,128)}, u32[]{:S(2)}) copy-start(f32[32,256]{1,0:T(8,128)} %get-tuple-element.41) | copy-start | bytes 98308
  194.1 4.3 %collective-permute-start.2 = (f32[1,24,1,256]{3,2,1,0:T(1,128)S(1)}, f32[1,24,1,256]{3,2,1,0:T(1,128)S(1)}, u32[]{:S(2)}, u32[]{:S(2)}) collective-permute-start(f32[1,24,1,256]{3,2,1,0:T(1,128)S(1)} %get-tuple-element.27), channel_id=1, source_target_pairs={{0,8},{8,16},{16,24},{24,32},{32,40},{40,48},{48,56},{56,64},{64,7... | collective-permute-start | bytes 73736 | tf_op jit(solution)/shard_map/ppermute | solution.py:32
  197.2 4.6 %collective-permute-start.3 = (f32[1,24,1,256]{3,2,1,0:T(1,128)S(1)}, f32[1,24,1,256]{3,2,1,0:T(1,128)S(1)}, u32[]{:S(2)}, u32[]{:S(2)}) collective-permute-start(f32[1,24,1,256]{3,2,1,0:T(1,128)S(1)} %get-tuple-element.28), channel_id=1, source_target_pairs={{8,0},{16,8},{24,16},{32,24},{40,32},{48,40},{56,48},{64,56},{72,6... | collective-permute-start | bytes 73736 | tf_op jit(solution)/shard_map/ppermute | solution.py:33
  202.0 17.5 %collective-permute-start.4 = (f32[1,24,34,1]{3,2,1,0:T(8,128)S(1)}, f32[1,24,34,1]{3,2,1,0:T(8,128)S(1)}, u32[]{:S(2)}, u32[]{:S(2)}) collective-permute-start(f32[1,24,34,1]{3,2,1,0:T(8,128)S(1)} %get-tuple-element.11), channel_id=1, source_target_pairs={{0,1},{1,2},{2,3},{3,4},{4,5},{5,6},{6,7},{8,9},{9,10},{10,11},{11... | collective-permute-start | bytes 9800 | tf_op jit(solution)/shard_map/ppermute | solution.py:32
  213.7 29.0 %collective-permute-start.5 = (f32[1,24,34,1]{3,2,1,0:T(8,128)S(1)}, f32[1,24,34,1]{3,2,1,0:T(8,128)S(1)}, u32[]{:S(2)}, u32[]{:S(2)}) collective-permute-start(f32[1,24,34,1]{3,2,1,0:T(8,128)S(1)} %get-tuple-element.12), channel_id=1, source_target_pairs={{1,0},{2,1},{3,2},{4,3},{5,4},{6,5},{7,6},{9,8},{10,9},{11,10},{12... | collective-permute-start | bytes 9800 | tf_op jit(solution)/shard_map/ppermute | solution.py:33
  252.0 35.8 %collective-permute-start.7 = (f32[3,24,16,128]{3,2,1,0:T(8,128)}, f32[3,24,16,128]{3,2,1,0:T(8,128)}, u32[]{:S(2)}, u32[]{:S(2)}) collective-permute-start(f32[3,24,16,128]{3,2,1,0:T(8,128)} %pad_maximum_fusion.21), channel_id=1, source_target_pairs={{0,8},{8,0},{16,24},{24,16},{32,40},{40,32},{48,56},{56,48},{64,72... | collective-permute-start | bytes 1769480 | tf_op jit(solution)/shard_map/ppermute | solution.py:17
  262.4 25.5 %copy-start.1 = (f32[1,24,16,128]{3,2,1,0:T(8,128)S(1)}, f32[1,24,16,128]{3,2,1,0:T(8,128)}, u32[]{:S(2)}) copy-start(f32[1,24,16,128]{3,2,1,0:T(8,128)} %get-tuple-element.21) | copy-start | bytes 589828
  262.4 25.5 %copy-start.2 = (f32[1,24,16,128]{3,2,1,0:T(8,128)S(1)}, f32[1,24,16,128]{3,2,1,0:T(8,128)}, u32[]{:S(2)}) copy-start(f32[1,24,16,128]{3,2,1,0:T(8,128)} %get-tuple-element.25) | copy-start | bytes 589828
  277.8 12.1 %collective-permute-start.6 = (f32[3,24,16,128]{3,2,1,0:T(8,128)}, f32[3,24,16,128]{3,2,1,0:T(8,128)S(1)}, u32[]{:S(2)}, u32[]{:S(2)}) collective-permute-start(f32[3,24,16,128]{3,2,1,0:T(8,128)} %get-tuple-element.35), channel_id=1, source_target_pairs={{0,8},{8,0},{16,24},{24,16},{32,40},{40,32},{48,56},{56,48},{64,72... | collective-permute-start | bytes 1769480 | tf_op jit(solution)/shard_map/ppermute | solution.py:17
  354.7 6.4 %copy-start.4 = (f32[32,256]{1,0:T(8,128)S(1)}, f32[32,256]{1,0:T(8,128)}, u32[]{:S(2)}) copy-start(f32[32,256]{1,0:T(8,128)} %multiply_subtract_fusion) | copy-start | bytes 98308
  363.3 4.4 %collective-permute-start.8 = (f32[1,24,1,256]{3,2,1,0:T(1,128)S(1)}, f32[1,24,1,256]{3,2,1,0:T(1,128)S(1)}, u32[]{:S(2)}, u32[]{:S(2)}) collective-permute-start(f32[1,24,1,256]{3,2,1,0:T(1,128)S(1)} %get-tuple-element.19), channel_id=1, source_target_pairs={{0,8},{8,16},{16,24},{24,32},{32,40},{40,48},{48,56},{56,64},{64,7... | collective-permute-start | bytes 73736 | tf_op jit(solution)/shard_map/ppermute | solution.py:32
  366.5 4.6 %collective-permute-start.9 = (f32[1,24,1,256]{3,2,1,0:T(1,128)S(1)}, f32[1,24,1,256]{3,2,1,0:T(1,128)S(1)}, u32[]{:S(2)}, u32[]{:S(2)}) collective-permute-start(f32[1,24,1,256]{3,2,1,0:T(1,128)S(1)} %get-tuple-element.20), channel_id=1, source_target_pairs={{8,0},{16,8},{24,16},{32,24},{40,32},{48,40},{56,48},{64,56},{72,6... | collective-permute-start | bytes 73736 | tf_op jit(solution)/shard_map/ppermute | solution.py:33
  371.4 17.6 %collective-permute-start.10 = (f32[1,24,34,1]{3,2,1,0:T(8,128)S(1)}, f32[1,24,34,1]{3,2,1,0:T(8,128)S(1)}, u32[]{:S(2)}, u32[]{:S(2)}) collective-permute-start(f32[1,24,34,1]{3,2,1,0:T(8,128)S(1)} %get-tuple-element.9), channel_id=1, source_target_pairs={{0,1},{1,2},{2,3},{3,4},{4,5},{5,6},{6,7},{8,9},{9,10},{10,11},{11... | collective-permute-start | bytes 9800 | tf_op jit(solution)/shard_map/ppermute | solution.py:32
  383.1 28.7 %collective-permute-start.11 = (f32[1,24,34,1]{3,2,1,0:T(8,128)S(1)}, f32[1,24,34,1]{3,2,1,0:T(8,128)S(1)}, u32[]{:S(2)}, u32[]{:S(2)}) collective-permute-start(f32[1,24,34,1]{3,2,1,0:T(8,128)S(1)} %get-tuple-element.10), channel_id=1, source_target_pairs={{1,0},{2,1},{3,2},{4,3},{5,4},{6,5},{7,6},{9,8},{10,9},{11,10},{12... | collective-permute-start | bytes 9800 | tf_op jit(solution)/shard_map/ppermute | solution.py:33
  (8 other events, 28.9 us)
Sparse Core Ops, SparseCore 0:
  116.0 66.4 all-reduce.4
  290.0 61.9 all-reduce.6
where the time goes:
time: 424 us; the launch traced here: 420 us
  local copies, waits for them, and re-layouts  133 us (31%)
  waiting for transfers between devices  95.4 us (22%)
  other arithmetic  69.1 us (16%)
  starting transfers between devices  47.3 us (11%)
  between operations  44.1 us (10%)
  blocking collectives  31.3 us (7%)
    dynamic_update_slice x12, local copies, waits for them, and re-layouts, local(): lax.dynamic_update_slice(gathered, existing + pieces[slot], (anchor, tops...  101 us
    ppermute x4, waiting for transfers between devices, padded_2(): after = lax.ppermute(leading, axis, down)  52.4 us
    psum x2, waiting for transfers between devices, spread(): return lax.psum(block, axis)  35.2 us
    all_gather x2, blocking collectives, local(): lax.all_gather(child_block[None], 'grid', axis=0, tiled=True)[1:]  31.3 us
    ppermute x4, starting transfers between devices, padded_2(): before = lax.ppermute(last, axis, up)  29.5 us
    reduce_sum x2, other arithmetic, block_sums(): values.reshape(shape[:-2] + (shape[-2] // 2, 2, shape[-1] // 2, 2))  14.3 us
    mul x2, other arithmetic, local(): keep_here[slot]  12.3 us
    ppermute x4, starting transfers between devices, partner(): return lax.ppermute(value, axis, pairs)  11.2 us
  transfers between devices with their start and end apart: 14, of which 8 were waited for; matrix products, arithmetic and copies ran while one was open for 37% of the time, Pallas kernels for 0%

commit v1 on v0

v1 whole, which is shorter than its diff:
```python
import functools

import jax
import jax.numpy as jnp
from jax import lax
from jax.experimental import pallas as pl
from jax.experimental.pallas import tpu as pltpu
from jax.sharding import PartitionSpec as P

NCLS = 3
LEV = 8
STEPS = 2
CR = 32
CC = 256
HR = 16
HC = 128
SLOTS = 3
relaxation = 0.125

CHUNKS = 4
NL = LEV // CHUNKS
NK = NL * NCLS
NKP = -(-NK // 8) * 8
ROWS = NK * CR
WIDE = -(-ROWS // 128) * 128
TRIPS = STEPS * CHUNKS
MESH = pl.DeviceIdType.MESH
F32 = jnp.float32
BF16 = jnp.bfloat16

NORTH, SOUTH, WEST, EAST, UP, DOWN_X, UP_X, DOWN = 0, 1, 2, 3, 4, 7, 8, 9
KINDS = 12


def iota(shape, dim):
    return lax.broadcasted_iota(jnp.int32, shape, dim)


def halves(x):
    high = x.astype(BF16)
    return high, (x - high.astype(F32)).astype(BF16)


def exact_dot(x, selector):
    high, low = halves(x)
    return jnp.dot(high, selector, preferred_element_type=F32) + jnp.dot(low, selector, preferred_element_type=F32)


def kernel(
    adjoint,
    sea_mask,
    diffusivity,
    aggregation,
    breakup,
    sponge,
    settling,
    partner_flip,
    row_offset,
    col_offset,
    out,
    state,
    flux,
    above,
    low_cols,
    high_cols,
    wet,
    cover,
    placed,
    edges,
    row_send,
    row_recv,
    col_send,
    col_recv,
    up_send,
    up_recv,
    up_cross,
    down_cross_send,
    down_cross_recv,
    down_send,
    down_recv,
    load_sem,
    store_sem,
    send_sem,
    recv_sem,
):
    grid = lax.axis_index("grid")
    row = lax.axis_index("gx")
    col = lax.axis_index("gy")
    rows = lax.axis_size("gx")
    cols = lax.axis_size("gy")
    is_parent = grid == 0
    is_child = grid > 0
    partner = row + 1 - 2 * lax.rem(row, 2)
    slot_of = grid - 1
    sides = (
        (NORTH, row > 0, {"gx": row - 1}),
        (SOUTH, row < rows - 1, {"gx": row + 1}),
        (WEST, col > 0, {"gy": col - 1}),
        (EAST, col < cols - 1, {"gy": col + 1}),
    )

    loads = [
        pltpu.make_async_copy(
            adjoint.at[0, pl.ds(c * LEV, LEV), :, pl.ds(h * HC, HC)], state.at[:, c, h], load_sem.at[c, h]
        )
        for c in range(NCLS)
        for h in range(2)
    ]
    for load in loads:
        load.start()

    row_recv[...] = jnp.zeros_like(row_recv)
    col_recv[...] = jnp.zeros_like(col_recv)

    barrier = pltpu.get_barrier_semaphore()

    def greet(device):
        pl.semaphore_signal(barrier, inc=1, device_id=device, device_id_type=MESH)

    for _, there, device in sides:

        @pl.when(there)
        def _():
            greet(device)

    @pl.when(is_parent)
    def _():
        for slot in range(SLOTS):
            greet({"grid": slot + 1})

    @pl.when(is_child)
    def _():
        greet({"grid": 0})

    placed[...] = jnp.zeros_like(placed)
    wet[...] = sea_mask[0].astype(F32)

    def one(flag):
        return jnp.where(flag, 1, 0)

    tops = [row_offset[g, row, col] for g in range(SLOTS)] + [row_offset[g, partner, col] for g in range(SLOTS)]
    lefts = [col_offset[g, row, col] for g in range(SLOTS)] + [col_offset[g, partner, col] for g in range(SLOTS)]
    flags = [1 - partner_flip[g, row, col] for g in range(SLOTS)] + [partner_flip[g, partner, col] for g in range(SLOTS)]

    @pl.when(is_parent)
    def _():
        row_ids = iota((CR, CC), 0)
        col_ids = iota((CR, CC), 1)
        total = jnp.zeros((CR, CC), F32)
        for top, left, flag in zip(tops, lefts, flags):
            inside = (row_ids >= top) & (row_ids < top + HR) & (col_ids >= left) & (col_ids < left + HC)
            total = total + jnp.where(inside, flag.astype(F32), 0.0)
        cover[...] = 1.0 - relaxation * total

    pl.semaphore_wait(
        barrier,
        one(row > 0) + one(row < rows - 1) + one(col > 0) + one(col < cols - 1) + jnp.where(is_parent, SLOTS, 1),
    )
    for load in loads:
        load.wait()

    def copy(source, target, kind, trip, device, landing=None):
        return pltpu.make_async_remote_copy(
            src_ref=source,
            dst_ref=target,
            send_sem=send_sem.at[trip, kind],
            recv_sem=recv_sem.at[trip, kind if landing is None else landing],
            device_id=device,
            device_id_type=MESH,
        )

    def up_copy(trip):
        return copy(up_send.at[trip], up_recv.at[trip, slot_of], UP, trip, {"grid": 0}, UP + slot_of)

    def up_arrival(trip, slot):
        return copy(up_send.at[trip], up_recv.at[trip, slot], UP, trip, {"grid": slot + 1}, UP + slot)

    def up_cross_copy(trip):
        return copy(up_recv.at[trip], up_cross.at[trip], UP_X, trip, {"gx": partner})

    def down_cross_copy(trip):
        return copy(down_cross_send.at[trip], down_cross_recv.at[trip], DOWN_X, trip, {"gx": partner})

    def down_copy(trip, slot):
        return copy(down_send.at[trip, slot], down_recv.at[trip], DOWN + slot, trip, {"grid": slot + 1}, DOWN)

    def down_arrival(trip):
        return copy(down_send.at[trip, 0], down_recv.at[trip], DOWN, trip, {"grid": 0}, DOWN)

    def halo_copy(trip, side, device):
        if side < WEST:
            return copy(row_send.at[trip, side], row_recv.at[trip, 1 - side], side, trip, device, 1 - side)
        return copy(col_send.at[trip, side - WEST], col_recv.at[trip, EAST - side], side, trip, device, WEST + EAST - side)

    def halo_arrival(trip, side, device):
        if side < WEST:
            return copy(row_send.at[trip, side], row_recv.at[trip, side], side, trip, device, side)
        return copy(col_send.at[trip, side - WEST], col_recv.at[trip, side - WEST], side, trip, device, side)

    def base_level(chunk):
        return LEV - NL * (chunk + 1)

    def full(level, c):
        return jnp.concatenate([state[level, c, 0], state[level, c, 1]], axis=1)

    def put(level, c, values):
        state[level, c, 0] = values[:, :HC]
        state[level, c, 1] = values[:, HC:]

    def cut(level, c, top, left):
        shift = lax.rem(HC - left, HC)
        low = pltpu.roll(state[level, c, 0, pl.ds(top, HR), :], shift, 1)
        high = pltpu.roll(state[level, c, 1, pl.ds(top, HR), :], shift, 1)
        return jnp.where(iota((HR, HC), 1) < HC - left, low, high)

    def send_up(trip, chunk):
        base = base_level(chunk)
        weights = sponge[0]

        def component(level, c):
            product = weights * full(base + level, c)
            at = (level * NCLS + c) * CR
            low_cols[pl.ds(at, CR), :] = product[:, :HC]
            high_cols[pl.ds(at, CR), :] = product[:, HC:]

        @pl.loop(0, NL)
        def _(level):
            for c in range(NCLS):
                component(level, c)

        half = ROWS // 2
        low = low_cols[pl.ds(0, half, stride=2), :] + low_cols[pl.ds(1, half, stride=2), :]
        high = high_cols[pl.ds(0, half, stride=2), :] + high_cols[pl.ds(1, half, stride=2), :]
        selector = (iota((CC, HC), 0) // 2 == iota((CC, HC), 1)).astype(F32).astype(BF16)
        sums = exact_dot(jnp.concatenate([low, high], axis=1), selector)
        up_send[trip] = sums.reshape(NK, HR, HC)
        up_copy(trip).start()

    def send_cross(trip, chunk):
        base = base_level(chunk)

        @pl.loop(0, NL)
        def _(level):
            for c in range(NCLS):
                for slot in range(SLOTS):
                    down_cross_send[trip, slot, level * NCLS + c] = cut(
                        base + level, c, tops[SLOTS + slot], lefts[SLOTS + slot]
                    )

        down_cross_copy(trip).start()

    def send_down(trip, chunk):
        base = base_level(chunk)
        down_cross_copy(trip).wait_recv()
        for slot in range(SLOTS):
            keep = flags[slot].astype(F32)

            @pl.loop(0, NL)
            def _(level):
                for c in range(NCLS):
                    values = cut(base + level, c, tops[slot], lefts[slot])
                    other = down_cross_recv[trip, slot, level * NCLS + c]
                    down_send[trip, slot, level * NCLS + c] = keep * values + (1.0 - keep) * other

            down_copy(trip, slot).start()

    def forward_up(trip):
        for slot in range(SLOTS):
            up_arrival(trip, slot).wait_recv()
        up_cross_copy(trip).start()

    def nest_parent(trip, chunk):
        base = base_level(chunk)
        up_cross_copy(trip).wait_recv()
        lanes = iota((8, HC), 1)

        @pl.loop(0, NL)
        def _(level):
            for c in range(NCLS):
                k = level * NCLS + c
                old = full(base + level, c) * cover[...]
                low = old[:, :HC].reshape(CR // 8, 8, HC)
                high = old[:, HC:].reshape(CR // 8, 8, HC)
                for n in range(2 * SLOTS):
                    source = up_recv if n < SLOTS else up_cross
                    placed[c, n, HR : HR + HR] = source[trip, n % SLOTS, k]
                    piece = placed[c, n, pl.ds(HR - tops[n], CR), :]
                    piece = pltpu.roll(piece, lax.rem(lefts[n], HC), 1).reshape(CR // 8, 8, HC)
                    flag = flags[n].astype(F32)
                    low = low + jnp.where(lanes >= lefts[n], flag, 0.0)[None] * piece
                    high = high + jnp.where(lanes < lefts[n], flag, 0.0)[None] * piece
                state[base + level, c, 0] = low.reshape(CR, HC)
                state[base + level, c, 1] = high.reshape(CR, HC)

    def nest_child(trip, chunk):
        base = base_level(chunk)
        down_arrival(trip).wait_recv()
        selector = jnp.where(iota((HC, CC), 1) // 2 == iota((HC, CC), 0), relaxation / 4.0, 0.0).astype(BF16)
        half = ROWS // 2
        spread = exact_dot(down_recv[trip].reshape(NK * HR, HC), selector)
        for start in (0, 1):
            low_cols[pl.ds(start, half, stride=2), :] = spread[:, :HC]
            high_cols[pl.ds(start, half, stride=2), :] = spread[:, HC:]
        kept = 1.0 - sponge[0]

        @pl.loop(0, NL)
        def _(level):
            for c in range(NCLS):
                at = (level * NCLS + c) * CR
                added = jnp.concatenate([low_cols[pl.ds(at, CR), :], high_cols[pl.ds(at, CR), :]], axis=1)
                put(base + level, c, kept * full(base + level, c) + added)

    def local_part(trip, chunk):
        base = base_level(chunk)

        @pl.loop(0, NL)
        def _(index):
            level = NL - 1 - index
            u0 = full(base + level, 0)
            u1 = full(base + level, 1)
            u2 = full(base + level, 2)
            agg = aggregation[0]
            brk = breakup[0]
            flocced = (
                (1.0 - agg) * u0 + agg * u1,
                brk * u0 + (1.0 - agg - brk) * u1 + agg * u2,
                brk * u1 + (1.0 - brk) * u2,
            )
            for c in range(NCLS):
                rate = settling[grid, c]
                value = wet[...] * ((1.0 - rate) * flocced[c] + rate * above[c])
                above[c] = flocced[c]
                outward = diffusivity[0] * value
                k = level * NCLS + c
                put(base + level, c, value - 4.0 * outward)
                flux[trip, k, 8 : 8 + CR] = outward
                row_send[trip, 0, pl.ds(k, 1), :] = outward[0:1, :]
                row_send[trip, 1, pl.ds(k, 1), :] = outward[CR - 1 : CR, :]

        selector = jnp.where(iota((8, CC), 1) == iota((8, CC), 0) * (CC - 1), 1.0, 0.0).astype(BF16)
        high, low = halves(flux[trip, :, 8 : 8 + CR].reshape(ROWS, CC))
        dims = (((1,), (1,)), ((), ()))
        ends = lax.dot_general(selector, high, dims, preferred_element_type=F32) + lax.dot_general(
            selector, low, dims, preferred_element_type=F32
        )
        if WIDE > ROWS:
            ends = jnp.concatenate([ends, jnp.zeros((8, WIDE - ROWS), F32)], axis=1)
        col_send[trip, 0] = ends[0:1]
        col_send[trip, 1] = ends[1:2]
        for side, there, device in sides:

            @pl.when(there)
            def _():
                halo_copy(trip, side, device).start()

    def stencil(trip, chunk):
        base = base_level(chunk)
        for side, there, device in sides:

            @pl.when(there)
            def _():
                halo_arrival(trip, side, device).wait_recv()

        kind = iota((8, WIDE), 0)
        west = jnp.broadcast_to(col_recv[trip, 0], (8, WIDE))
        east = jnp.broadcast_to(col_recv[trip, 1], (8, WIDE))
        west_high = west.astype(BF16).astype(F32)
        east_high = east.astype(BF16).astype(F32)
        parts = jnp.where(
            kind == 0,
            west_high,
            jnp.where(kind == 1, west - west_high, jnp.where(kind == 2, east_high, jnp.where(kind == 3, east - east_high, 0.0))),
        )
        target = iota((8, CC), 0)
        lane = iota((8, CC), 1)
        selector = jnp.where(((target < 2) & (lane == 0)) | ((target >= 2) & (target < 4) & (lane == CC - 1)), 1.0, 0.0)
        edges[...] = jnp.dot(parts.T.astype(BF16), selector.astype(BF16), preferred_element_type=F32)

        @pl.loop(0, NL)
        def _(level):
            lane_ids = iota((CR, CC), 1)
            for c in range(NCLS):
                k = level * NCLS + c
                flux[trip, k, 7:8] = row_recv[trip, 0, pl.ds(k, 1), :]
                flux[trip, k, 8 + CR : 9 + CR] = row_recv[trip, 1, pl.ds(k, 1), :]
                middle = flux[trip, k, 8 : 8 + CR]
                left = jnp.where(lane_ids > 0, pltpu.roll(middle, 1, 1), 0.0)
                right = jnp.where(lane_ids < CC - 1, pltpu.roll(middle, CC - 1, 1), 0.0)
                put(
                    base + level,
                    c,
                    full(base + level, c)
                    + flux[trip, k, 7 : 7 + CR]
                    + flux[trip, k, 9 : 9 + CR]
                    + left
                    + right
                    + edges[pl.ds(k * CR, CR), :],
                )

    def first_sends(trip, chunk):
        @pl.when(is_parent)
        def _():
            send_cross(trip, chunk)

        @pl.when(is_child)
        def _():
            send_up(trip, chunk)

    def stores(chunk):
        base = base_level(chunk)
        return [
            pltpu.make_async_copy(
                state.at[pl.ds(base, NL), c, h],
                out.at[0, pl.ds(c * LEV + base, NL), :, pl.ds(h * HC, HC)],
                store_sem.at[chunk, c, h],
            )
            for c in range(NCLS)
            for h in range(2)
        ]

    @pl.loop(0, CHUNKS)
    def _(chunk):
        first_sends(chunk, chunk)

    for step in range(STEPS):
        start = step * CHUNKS

        @pl.when(is_parent)
        def _():
            @pl.loop(0, CHUNKS)
            def _(chunk):
                send_down(start + chunk, chunk)
                forward_up(start + chunk)

        above[...] = jnp.zeros_like(above)

        @pl.loop(0, CHUNKS)
        def _(chunk):
            @pl.when(is_parent)
            def _():
                nest_parent(start + chunk, chunk)

            @pl.when(is_child)
            def _():
                nest_child(start + chunk, chunk)

            local_part(start + chunk, chunk)

        @pl.loop(0, CHUNKS)
        def _(chunk):
            stencil(start + chunk, chunk)
            if step + 1 < STEPS:
                first_sends(start + CHUNKS + chunk, chunk)
            else:
                for store in stores(chunk):
                    store.start()

    @pl.loop(0, TRIPS)
    def _(trip):
        for side, there, device in sides:

            @pl.when(there)
            def _():
                halo_copy(trip, side, device).wait_send()

        @pl.when(is_parent)
        def _():
            down_cross_copy(trip).wait_send()
            up_cross_copy(trip).wait_send()
            for slot in range(SLOTS):
                down_copy(trip, slot).wait_send()

        @pl.when(is_child)
        def _():
            up_copy(trip).wait_send()

    @pl.loop(0, CHUNKS)
    def _(chunk):
        for store in stores(chunk):
            store.wait()


def local(*args):
    vmem = pl.BlockSpec(memory_space=pltpu.VMEM)
    smem = pl.BlockSpec(memory_space=pltpu.SMEM)
    hbm = pl.BlockSpec(memory_space=pl.ANY)
    return pl.pallas_call(
        kernel,
        out_shape=jax.ShapeDtypeStruct((1, NCLS * LEV, CR, CC), F32),
        in_specs=[hbm] + [vmem] * 5 + [smem] * 4,
        out_specs=hbm,
        scratch_shapes=[
            pltpu.VMEM((LEV, NCLS, 2, CR, HC), F32),
            pltpu.VMEM((TRIPS, NK, CR + 16, CC), F32),
            pltpu.VMEM((NCLS, CR, CC), F32),
            pltpu.VMEM((ROWS, HC), F32),
            pltpu.VMEM((ROWS, HC), F32),
            pltpu.VMEM((CR, CC), F32),
            pltpu.VMEM((CR, CC), F32),
            pltpu.VMEM((NCLS, 2 * SLOTS, 3 * HR, HC), F32),
            pltpu.VMEM((WIDE, CC), F32),
            pltpu.VMEM((TRIPS, 2, NKP, CC), F32),
            pltpu.VMEM((TRIPS, 2, NKP, CC), F32),
            pltpu.VMEM((TRIPS, 2, 1, WIDE), F32),
            pltpu.VMEM((TRIPS, 2, 1, WIDE), F32),
            pltpu.VMEM((TRIPS, NK, HR, HC), F32),
            pltpu.VMEM((TRIPS, SLOTS, NK, HR, HC), F32),
            pltpu.VMEM((TRIPS, SLOTS, NK, HR, HC), F32),
            pltpu.VMEM((TRIPS, SLOTS, NK, HR, HC), F32),
            pltpu.VMEM((TRIPS, SLOTS, NK, HR, HC), F32),
            pltpu.VMEM((TRIPS, SLOTS, NK, HR, HC), F32),
            pltpu.VMEM((TRIPS, NK, HR, HC), F32),
            pltpu.SemaphoreType.DMA((NCLS, 2)),
            pltpu.SemaphoreType.DMA((CHUNKS, NCLS, 2)),
            pltpu.SemaphoreType.DMA((TRIPS, KINDS)),
            pltpu.SemaphoreType.DMA((TRIPS, KINDS)),
        ],
        compiler_params=pltpu.CompilerParams(
            collective_id=0, has_side_effects=True, vmem_limit_bytes=40 * 1024 * 1024
        ),
        name="nested_steps",
    )(*args)


def solution(mesh):
    tile = P("grid", "gx", "gy")
    in_specs = (P("grid", None, "gx", "gy"),) + (tile,) * 5 + (P(),) * 4
    return jax.shard_map(
        local, mesh=mesh, in_specs=in_specs, out_specs=P("grid", None, "gx", "gy"), check_vma=False
    )
```

time: 424 us -> 80.2 us (0.19)
  local copies, waits for them, and re-layouts: 133 us -> 5.91 us
  waiting for transfers between devices: 95.4 us -> 0 us
  Pallas kernels: 0 us -> 73.7 us
  other arithmetic: 69.1 us -> 0 us
  starting transfers between devices: 47.3 us -> 0 us
  between operations: 44.1 us -> 0.04 us
  blocking collectives: 31.3 us -> 0 us
    dynamic_update_slice x12 -> x0, local copies, waits for them, and re-layouts: 101 us -> none  [local(): lax.dynamic_update_slice(gathered, existing + pieces[slot], (anchor, tops...]
    pallas_call x0 -> x1, Pallas kernels: none -> 73.7 us  [local(): pl.pallas_call(kernel, out_shape=jax.ShapeDtypeStruct((1, NCLS * LEV, CR,...]
    ppermute x12 -> x0, waiting for transfers between devices: 60.2 us -> none  [the longest x4 52.4 us: padded_2(): after = lax.ppermute(leading, axis, down)]
    ppermute x12 -> x0, starting transfers between devices: 47.3 us -> none  [the longest x4 29.5 us: padded_2(): before = lax.ppermute(last, axis, up)]
    psum x2 -> x0, waiting for transfers between devices: 35.2 us -> none  [spread(): return lax.psum(block, axis)]
    all_gather x2 -> x0, blocking collectives: 31.3 us -> none  [local(): lax.all_gather(child_block[None], 'grid', axis=0, tiled=True)[1:]]
    mul x10 -> x0, other arithmetic: 17.1 us -> none  [the longest x2 12.3 us: local(): keep_here[slot]]
    reduce_sum x2 -> x0, other arithmetic: 14.3 us -> none  [block_sums(): values.reshape(shape[:-2] + (shape[-2] // 2, 2, shape[-1] // 2, 2))]
  transfers between devices with their start and end apart: 14 -> 0, of which waited for: 8 -> 0; matrix products, arithmetic and copies ran while one was open for 37% -> 0% of each run, Pallas kernels for 0% -> 0%
where the time goes in v1:
time: 80.2 us; the launch traced here: 79.7 us
  Pallas kernels  73.7 us (92%)
  local copies, waits for them, and re-layouts  5.91 us (7%)
    pallas_call x1, Pallas kernels, local(): pl.pallas_call(kernel, out_shape=jax.ShapeDtypeStruct((1, NCLS * LEV, CR,...  73.7 us
    unnamed x18, local copies, waits for them, and re-layouts  5.91 us

profile of v1, /device:TPU:1, one launch (start us, length us, event | category | flops | bytes accessed | tf_op | source)
XLA Modules:
  0.0 79.7 jit_solution(6015696633044622651)
XLA Ops:
  0.0 0.0 copy-start.3
  0.0 0.8 copy.11.partner_flip
  0.8 0.0 copy-start.1
  0.8 0.0 copy-start.2
  0.8 0.8 copy.12.row_offset
  1.6 0.0 copy-start.6
  1.6 0.8 copy.13.col_offset
  2.4 0.0 copy-done.3
  2.4 0.0 copy-done.1
  2.4 0.0 copy-done.2
  2.4 0.0 copy-done.6
  2.4 0.0 copy-start
  2.4 1.1 %copy-done = f32[1,24,32,256]{3,2,1,0:T(8,128)S(1)} copy-done((f32[1,24,32,256]{3,2,1,0:T(8,128)S(1)}, f32[1,24,32,256]{3,2,1,0:T(8,128)}, u32[]{:S(2)}) %copy-start) | copy-done | bytes 786456
  3.5 0.0 copy-start.4
  3.5 0.8 copy-done.4
  4.3 0.0 copy-start.5
  4.3 0.8 copy-done.5
  5.1 73.7 %nested_steps.1 = f32[1,24,32,256]{3,2,1,0:T(8,128)S(1)} custom-call(f32[1,24,32,256]{3,2,1,0:T(8,128)S(1)} %copy-done, s32[1,32,256]{2,1,0:T(8,128)S(1)} %copy-done.1, f32[1,32,256]{2,1,0:T(8,128)S(1)} %copy-done.2, f32[1,32,256]{2,1,0:T(8,128)S(1)} %copy-done.3, f32[1,32,256]{2,1,0:T(8,128)S(1)} %copy-done.4, f32[1,32,256]{2,1,0:T(8,128)S(1)} %copy-done.5, ...), custom_call_target="tpu_custom_call" | custom-call | tf_op jit(solution)/shard_map/nested_steps/pallas_call | solution.py:487
  78.8 0.9 %copy.15 = f32[1,24,32,256]{3,2,1,0:T(8,128)} copy(f32[1,24,32,256]{3,2,1,0:T(8,128)S(1)} %nested_steps.1) | data formatting | bytes 1572864
Async XLA Ops:
  0.0 2.4 %copy-start.3 = (f32[1,32,256]{2,1,0:T(8,128)S(1)}, f32[1,32,256]{2,1,0:T(8,128)}, u32[]{:S(2)}) copy-start(f32[1,32,256]{2,1,0:T(8,128)} %aggregation.1) | copy-start | bytes 98308
  0.8 1.6 %copy-start.1 = (s32[1,32,256]{2,1,0:T(8,128)S(1)}, s32[1,32,256]{2,1,0:T(8,128)}, u32[]{:S(2)}) copy-start(s32[1,32,256]{2,1,0:T(8,128)} %sea_mask.1) | copy-start | bytes 98308
  0.8 1.6 %copy-start.2 = (f32[1,32,256]{2,1,0:T(8,128)S(1)}, f32[1,32,256]{2,1,0:T(8,128)}, u32[]{:S(2)}) copy-start(f32[1,32,256]{2,1,0:T(8,128)} %diffusivity.1) | copy-start | bytes 98308
  1.6 0.8 %copy-start.6 = (f32[4,3]{1,0:T(4,128)S(1)}, f32[4,3]{1,0:T(4,128)}, u32[]{:S(2)}) copy-start(f32[4,3]{1,0:T(4,128)} %settling.1) | copy-start | bytes 148
  2.4 1.1 %copy-start = (f32[1,24,32,256]{3,2,1,0:T(8,128)S(1)}, f32[1,24,32,256]{3,2,1,0:T(8,128)}, u32[]{:S(2)}) copy-start(f32[1,24,32,256]{3,2,1,0:T(8,128)} %adjoint.1) | copy-start | bytes 2359300
  3.5 0.8 copy-start.4
  4.3 0.8 copy-start.5

commit v2 on v1

v2 whole, which is shorter than its diff:
```python
import functools

import jax
import jax.numpy as jnp
from jax import lax
from jax.experimental import pallas as pl
from jax.experimental.pallas import tpu as pltpu
from jax.sharding import PartitionSpec as P

NCLS = 3
LEV = 8
STEPS = 2
CR = 32
CC = 256
HR = 16
HC = 128
SLOTS = 3
relaxation = 0.125

CHUNKS = 8
NL = LEV // CHUNKS
NK = NL * NCLS
NKP = -(-NK // 8) * 8
ROWS = NK * CR
WIDE = NL * HC
TRIPS = STEPS * CHUNKS
MESH = pl.DeviceIdType.MESH
F32 = jnp.float32
BF16 = jnp.bfloat16

NORTH, SOUTH, WEST, EAST, UP, UP_X, RELAY, DOWN_X, DOWN = 0, 1, 2, 3, 4, 7, 8, 9, 10
KINDS = 11
LAG = 3
LEAD_SEND, LEAD_ANSWER, LEAD_RELAY = CHUNKS - LAG, 2, 4


def iota(shape, dim):
    return lax.broadcasted_iota(jnp.int32, shape, dim)


def halves(x):
    high = x.astype(BF16)
    return high, (x - high.astype(F32)).astype(BF16)


def exact_dot(x, selector):
    high, low = halves(x)
    return jnp.dot(high, selector, preferred_element_type=F32) + jnp.dot(low, selector, preferred_element_type=F32)


def kernel(
    adjoint,
    sea_mask_in,
    diffusivity_in,
    aggregation_in,
    breakup_in,
    sponge_in,
    settling_in,
    partner_flip_in,
    row_offset_in,
    col_offset_in,
    out,
    sea_mask,
    diffusivity,
    aggregation,
    breakup,
    sponge,
    settling,
    partner_flip,
    row_offset,
    col_offset,
    state,
    flux,
    above,
    low_cols,
    high_cols,
    wet,
    cover,
    placed,
    row_send,
    row_recv,
    col_send,
    col_recv,
    up_send,
    up_recv,
    relayed,
    up_cross,
    down_cross_send,
    down_cross_recv,
    down_send,
    down_recv,
    field_sem,
    load_sem,
    store_sem,
    send_sem,
    recv_sem,
):
    grid = lax.axis_index("grid")
    row = lax.axis_index("gx")
    col = lax.axis_index("gy")
    rows = lax.axis_size("gx")
    cols = lax.axis_size("gy")
    is_parent = grid == 0
    is_child = grid > 0
    is_relay = grid == SLOTS
    behind = lax.rem(col + cols - 2, cols)
    ahead = lax.rem(col + 2, cols)
    partner = row + 1 - 2 * lax.rem(row, 2)
    slot_of = grid - 1
    sides = (
        (NORTH, {"gx": lax.rem(row + rows - 1, rows)}),
        (SOUTH, {"gx": lax.rem(row + 1, rows)}),
        (WEST, {"gy": lax.rem(col + cols - 1, cols)}),
        (EAST, {"gy": lax.rem(col + 1, cols)}),
    )
    inner = [
        jnp.where(joint, 0.0, 1.0) for joint in (row == 0, row == rows - 1, col == 0, col == cols - 1)
    ]

    fields = [
        pltpu.make_async_copy(source, target, field_sem.at[n])
        for n, (source, target) in enumerate(
            (
                (partner_flip_in, partner_flip),
                (row_offset_in, row_offset),
                (col_offset_in, col_offset),
                (settling_in, settling),
                (sponge_in, sponge),
                (sea_mask_in, sea_mask),
                (diffusivity_in, diffusivity),
                (aggregation_in, aggregation),
                (breakup_in, breakup),
            )
        )
    ]
    loads = [
        pltpu.make_async_copy(
            adjoint.at[0, pl.ds(c * LEV, LEV), :, pl.ds(h * HC, HC)], state.at[:, c, h], load_sem.at[c, h]
        )
        for c in range(NCLS)
        for h in range(2)
    ]
    for load in fields[:3] + loads + fields[3:]:
        load.start()

    barrier = pltpu.get_barrier_semaphore()

    def greet(device):
        pl.semaphore_signal(barrier, inc=1, device_id=device, device_id_type=MESH)

    for _, device in sides:
        greet(device)

    @pl.when(is_parent)
    def _():
        for slot in range(SLOTS):
            greet({"grid": slot + 1})
        greet({"grid": SLOTS, "gx": partner, "gy": behind})
        greet({"grid": SLOTS, "gy": behind})

    @pl.when(is_child)
    def _():
        greet({"grid": 0})

    @pl.when(is_relay)
    def _():
        greet({"grid": 0, "gx": partner, "gy": ahead})
        greet({"grid": 0, "gy": ahead})

    placed[...] = jnp.zeros_like(placed)
    for load in fields:
        load.wait()
    wet[...] = sea_mask[0].astype(F32)

    tops = [row_offset[g, col, row] for g in range(SLOTS)] + [row_offset[g, col, partner] for g in range(SLOTS)]
    lefts = [col_offset[g, col, row] for g in range(SLOTS)] + [col_offset[g, col, partner] for g in range(SLOTS)]
    flags = [1 - partner_flip[g, col, row] for g in range(SLOTS)] + [partner_flip[g, col, partner] for g in range(SLOTS)]

    @pl.when(is_parent)
    def _():
        row_ids = iota((CR, CC), 0)
        col_ids = iota((CR, CC), 1)
        total = jnp.zeros((CR, CC), F32)
        for top, left, flag in zip(tops, lefts, flags):
            inside = (row_ids >= top) & (row_ids < top + HR) & (col_ids >= left) & (col_ids < left + HC)
            total = total + jnp.where(inside, flag.astype(F32), 0.0)
        cover[...] = 1.0 - relaxation * total

    pl.semaphore_wait(
        barrier,
        4 + jnp.where(is_parent, SLOTS + 2, 1) + jnp.where(is_relay, 2, 0),
    )
    for load in loads:
        load.wait()

    def copy(source, target, kind, trip, device, landing=None):
        return pltpu.make_async_remote_copy(
            src_ref=source,
            dst_ref=target,
            send_sem=send_sem.at[kind],
            recv_sem=recv_sem.at[trip, kind if landing is None else landing],
            device_id=device,
            device_id_type=MESH,
        )

    def up_copy(trip):
        return copy(up_send.at[trip], up_recv.at[trip, slot_of], UP, trip, {"grid": 0}, UP + slot_of)

    def up_arrival(trip, slot):
        return copy(up_send.at[trip], up_recv.at[trip, slot], UP, trip, {"grid": slot + 1}, UP + slot)

    def up_cross_copy(trip):
        return copy(up_recv.at[trip], up_cross.at[trip], UP_X, trip, {"gx": partner})

    def relay_copy(trip):
        return copy(
            down_cross_send.at[trip], relayed.at[trip], RELAY, trip, {"grid": SLOTS, "gx": partner, "gy": behind}
        )

    def down_cross_copy(trip):
        return copy(relayed.at[trip], down_cross_recv.at[trip], DOWN_X, trip, {"grid": 0, "gy": ahead})

    def down_copy(trip, slot):
        return copy(down_send.at[trip, slot], down_recv.at[trip], DOWN, trip, {"grid": slot + 1})

    def down_arrival(trip):
        return copy(down_send.at[trip, 0], down_recv.at[trip], DOWN, trip, {"grid": 0}, DOWN)

    def halo_copy(trip, side, device):
        if side < WEST:
            return copy(row_send.at[trip, side], row_recv.at[trip, 1 - side], side, trip, device, 1 - side)
        return copy(col_send.at[trip, side - WEST], col_recv.at[trip, EAST - side], side, trip, device, WEST + EAST - side)

    def halo_arrival(trip, side, device):
        if side < WEST:
            return copy(row_send.at[trip, side], row_recv.at[trip, side], side, trip, device, side)
        return copy(col_send.at[trip, side - WEST], col_recv.at[trip, side - WEST], side, trip, device, side)

    def base_level(chunk):
        return LEV - NL * (chunk + 1)

    def full(level, c):
        return jnp.concatenate([state[level, c, 0], state[level, c, 1]], axis=1)

    def put(level, c, values):
        state[level, c, 0] = values[:, :HC]
        state[level, c, 1] = values[:, HC:]

    def cut(level, c, top, left):
        low = state[level, c, 0, pl.ds(top, HR), :]
        high = state[level, c, 1, pl.ds(top, HR), :]
        return pltpu.roll(jnp.where(iota((HR, HC), 1) >= left, low, high), lax.rem(HC - left, HC), 1)

    def send_up(trip, chunk):
        base = base_level(chunk)
        weights = sponge[0]

        def component(level, c):
            product = weights * full(base + level, c)
            at = (level * NCLS + c) * CR
            low_cols[pl.ds(at, CR), :] = product[:, :HC]
            high_cols[pl.ds(at, CR), :] = product[:, HC:]

        for level in range(NL):
            for c in range(NCLS):
                component(level, c)

        half = ROWS // 2
        low = low_cols[pl.ds(0, half, stride=2), :] + low_cols[pl.ds(1, half, stride=2), :]
        high = high_cols[pl.ds(0, half, stride=2), :] + high_cols[pl.ds(1, half, stride=2), :]
        selector = (iota((CC, HC), 0) // 2 == iota((CC, HC), 1)).astype(F32).astype(BF16)
        sums = exact_dot(jnp.concatenate([low, high], axis=1), selector)
        up_send[trip] = sums.reshape(NK, HR, HC)
        up_copy(trip).start()

    def send_cross(trip, chunk):
        base = base_level(chunk)

        for level in range(NL):
            for c in range(NCLS):
                for slot in range(SLOTS):
                    down_cross_send[trip, slot, level * NCLS + c] = cut(
                        base + level, c, tops[SLOTS + slot], lefts[SLOTS + slot]
                    )

        relay_copy(trip).start()

    def send_down(trip, chunk):
        base = base_level(chunk)
        down_cross_copy(trip).wait_recv()
        for slot in range(SLOTS):
            keep = flags[slot].astype(F32)

            for level in range(NL):
                for c in range(NCLS):
                    values = cut(base + level, c, tops[slot], lefts[slot])
                    other = down_cross_recv[trip, slot, level * NCLS + c]
                    down_send[trip, slot, level * NCLS + c] = keep * values + (1.0 - keep) * other

            down_copy(trip, slot).start()

    def forward_up(trip):
        for slot in range(SLOTS):
            up_arrival(trip, slot).wait_recv()
        up_cross_copy(trip).start()

    def relay(trip):
        relay_copy(trip).wait_recv()
        down_cross_copy(trip).start()

    def nest_parent(trip, chunk):
        base = base_level(chunk)
        up_cross_copy(trip).wait_recv()
        lanes = iota((8, HC), 1)

        for level in range(NL):
            for c in range(NCLS):
                k = level * NCLS + c
                old = full(base + level, c) * cover[...]
                low = old[:, :HC].reshape(CR // 8, 8, HC)
                high = old[:, HC:].reshape(CR // 8, 8, HC)
                for n in range(2 * SLOTS):
                    source = up_recv if n < SLOTS else up_cross
                    placed[c, n, HR : HR + HR] = pltpu.roll(source[trip, n % SLOTS, k], lax.rem(lefts[n], HC), 1)
                    piece = placed[c, n, pl.ds(HR - tops[n], CR), :].reshape(CR // 8, 8, HC)
                    flag = flags[n].astype(F32)
                    low = low + jnp.where(lanes >= lefts[n], flag, 0.0)[None] * piece
                    high = high + jnp.where(lanes < lefts[n], flag, 0.0)[None] * piece
                state[base + level, c, 0] = low.reshape(CR, HC)
                state[base + level, c, 1] = high.reshape(CR, HC)

    def nest_child(trip, chunk):
        base = base_level(chunk)
        down_arrival(trip).wait_recv()
        selector = jnp.where(iota((HC, CC), 1) // 2 == iota((HC, CC), 0), relaxation / 4.0, 0.0).astype(BF16)
        half = ROWS // 2
        spread = exact_dot(down_recv[trip].reshape(NK * HR, HC), selector)
        for start in (0, 1):
            low_cols[pl.ds(start, half, stride=2), :] = spread[:, :HC]
            high_cols[pl.ds(start, half, stride=2), :] = spread[:, HC:]
        kept = 1.0 - sponge[0]

        for level in range(NL):
            for c in range(NCLS):
                at = (level * NCLS + c) * CR
                added = jnp.concatenate([low_cols[pl.ds(at, CR), :], high_cols[pl.ds(at, CR), :]], axis=1)
                put(base + level, c, kept * full(base + level, c) + added)

    def local_part(trip, chunk):
        base = base_level(chunk)

        @pl.when(chunk == 0)
        def _():
            above[...] = jnp.zeros_like(above)

        for level in reversed(range(NL)):
            u0 = full(base + level, 0)
            u1 = full(base + level, 1)
            u2 = full(base + level, 2)
            agg = aggregation[0]
            brk = breakup[0]
            flocced = (
                (1.0 - agg) * u0 + agg * u1,
                brk * u0 + (1.0 - agg - brk) * u1 + agg * u2,
                brk * u1 + (1.0 - brk) * u2,
            )
            columns = []
            for c in range(NCLS):
                rate = settling[grid, c]
                value = wet[...] * ((1.0 - rate) * flocced[c] + rate * above[c])
                above[c] = flocced[c]
                outward = diffusivity[0] * value
                k = level * NCLS + c
                put(base + level, c, value - 4.0 * outward)
                flux[trip, k, 8 : 8 + CR] = outward
                row_send[trip, 0, pl.ds(k, 1), :] = outward[0:1, :]
                row_send[trip, 1, pl.ds(k, 1), :] = outward[CR - 1 : CR, :]
                columns.append(jnp.where(iota((CR, HC), 1) < HC // 2, outward[:, :HC], outward[:, HC:]))

            square = jnp.concatenate(columns + [jnp.zeros((HC - NCLS * CR, HC), F32)], axis=0).T
            col_send[trip, 0, :, level * HC : (level + 1) * HC] = square[0:1]
            col_send[trip, 1, :, level * HC : (level + 1) * HC] = square[HC - 1 : HC]


        for side, device in sides:
            halo_copy(trip, side, device).start()

    def stencil(trip, chunk):
        base = base_level(chunk)
        for side, device in sides:
            halo_arrival(trip, side, device).wait_recv()

        for level in range(NL):
            for c in range(NCLS):
                k = level * NCLS + c
                flux[trip, k, 7:8] = inner[NORTH] * row_recv[trip, 0, pl.ds(k, 1), :]
                flux[trip, k, 8 + CR : 9 + CR] = inner[SOUTH] * row_recv[trip, 1, pl.ds(k, 1), :]
            west = inner[WEST] * col_recv[trip, 0, :, level * HC : (level + 1) * HC]
            east = inner[EAST] * col_recv[trip, 1, :, level * HC : (level + 1) * HC]
            kind = iota((HC, HC), 0)
            square = jnp.where(kind == 0, west, jnp.where(kind == HC - 1, east, 0.0)).T
            lanes = iota((CR, HC), 1)
            lane_ids = iota((CR, CC), 1)
            results = []
            for c in range(NCLS):
                k = level * NCLS + c
                middle = flux[trip, k, 8 : 8 + CR]
                left = jnp.where(lane_ids > 0, pltpu.roll(middle, 1, 1), 0.0)
                right = jnp.where(lane_ids < CC - 1, pltpu.roll(middle, CC - 1, 1), 0.0)
                ends = square[c * CR : (c + 1) * CR]
                ends = jnp.concatenate(
                    [jnp.where(lanes < HC // 2, ends, 0.0), jnp.where(lanes >= HC // 2, ends, 0.0)], axis=1
                )
                results.append(
                    full(base + level, c)
                    + flux[trip, k, 7 : 7 + CR]
                    + flux[trip, k, 9 : 9 + CR]
                    + left
                    + right
                    + ends
                )
            for c in range(NCLS):
                put(base + level, c, results[c])

    def first_sends(trip, chunk):
        @pl.when(is_parent)
        def _():
            send_cross(trip, chunk)

        @pl.when(is_child)
        def _():
            send_up(trip, chunk)

    def stores(chunk):
        base = base_level(chunk)
        return [
            pltpu.make_async_copy(
                state.at[base + level, :, h],
                out.at[0, :, base + level, :, pl.ds(h * HC, HC)],
                store_sem.at[chunk, level, h],
            )
            for level in range(NL)
            for h in range(2)
        ]

    def in_range(trip):
        return (trip >= 0) & (trip < TRIPS)

    @pl.loop(0, TRIPS + LEAD_SEND + LAG)
    def _(tick):
        now = tick - LEAD_SEND

        @pl.when(now >= LAG)
        def _():
            stencil(now - LAG, lax.rem(now - LAG + CHUNKS, CHUNKS))

        @pl.when(now >= CHUNKS + LAG)
        def _():
            for store in stores(now - LAG - CHUNKS):
                store.start()

        sending = now + LEAD_SEND

        @pl.when(sending < TRIPS)
        def _():
            first_sends(sending, lax.rem(sending, CHUNKS))

        answering = now + LEAD_ANSWER

        @pl.when(is_parent & in_range(answering))
        def _():
            send_down(answering, lax.rem(answering + CHUNKS, CHUNKS))
            forward_up(answering)

        relaying = now + LEAD_RELAY

        @pl.when(is_relay & in_range(relaying))
        def _():
            relay(relaying)

        @pl.when(in_range(now))
        def _():
            chunk = lax.rem(now + CHUNKS, CHUNKS)

            @pl.when(is_parent)
            def _():
                nest_parent(now, chunk)

            @pl.when(is_child)
            def _():
                nest_child(now, chunk)

            local_part(now, chunk)

    def sent(source, kind, device):
        copy(source, source, kind, 0, device).wait_send()

    for side, device in sides:
        sent(row_send.at[:, side] if side < WEST else col_send.at[:, side - WEST], side, device)

    @pl.when(is_parent)
    def _():
        sent(down_cross_send, RELAY, {"gx": partner})
        sent(up_recv, UP_X, {"gx": partner})
        sent(down_send, DOWN, {"gx": partner})

    @pl.when(is_child)
    def _():
        sent(up_send, UP, {"grid": 0})

    @pl.when(is_relay)
    def _():
        sent(relayed, DOWN_X, {"grid": 0})

    @pl.loop(0, CHUNKS)
    def _(chunk):
        for store in stores(chunk):
            store.wait()


def local(adjoint, sea_mask, diffusivity, aggregation, breakup, sponge, settling, *tables):
    hbm = pl.BlockSpec(memory_space=pl.ANY)
    return pl.pallas_call(
        kernel,
        out_shape=jax.ShapeDtypeStruct((1, NCLS, LEV, CR, CC), F32),
        in_specs=[hbm] * 10,
        out_specs=hbm,
        scratch_shapes=[
            pltpu.VMEM((1, CR, CC), jnp.int32),
            pltpu.VMEM((1, CR, CC), F32),
            pltpu.VMEM((1, CR, CC), F32),
            pltpu.VMEM((1, CR, CC), F32),
            pltpu.VMEM((1, CR, CC), F32),
            pltpu.SMEM(settling.shape, F32),
        ]
        + [pltpu.SMEM((t.shape[0], t.shape[2], t.shape[1]), jnp.int32) for t in tables]
        + [
            pltpu.VMEM((LEV, NCLS, 2, CR, HC), F32),
            pltpu.VMEM((TRIPS, NK, CR + 16, CC), F32),
            pltpu.VMEM((NCLS, CR, CC), F32),
            pltpu.VMEM((ROWS, HC), F32),
            pltpu.VMEM((ROWS, HC), F32),
            pltpu.VMEM((CR, CC), F32),
            pltpu.VMEM((CR, CC), F32),
            pltpu.VMEM((NCLS, 2 * SLOTS, 3 * HR, HC), F32),
            pltpu.VMEM((TRIPS, 2, NKP, CC), F32),
            pltpu.VMEM((TRIPS, 2, NKP, CC), F32),
            pltpu.VMEM((TRIPS, 2, 1, WIDE), F32),
            pltpu.VMEM((TRIPS, 2, 1, WIDE), F32),
            pltpu.VMEM((TRIPS, NK, HR, HC), F32),
            pltpu.VMEM((TRIPS, SLOTS, NK, HR, HC), F32),
            pltpu.VMEM((TRIPS, SLOTS, NK, HR, HC), F32),
            pltpu.VMEM((TRIPS, SLOTS, NK, HR, HC), F32),
            pltpu.VMEM((TRIPS, SLOTS, NK, HR, HC), F32),
            pltpu.VMEM((TRIPS, SLOTS, NK, HR, HC), F32),
            pltpu.VMEM((TRIPS, SLOTS, NK, HR, HC), F32),
            pltpu.VMEM((TRIPS, NK, HR, HC), F32),
            pltpu.SemaphoreType.DMA((9,)),
            pltpu.SemaphoreType.DMA((NCLS, 2)),
            pltpu.SemaphoreType.DMA((CHUNKS, NL, 2)),
            pltpu.SemaphoreType.DMA((KINDS,)),
            pltpu.SemaphoreType.DMA((TRIPS, KINDS)),
        ],
        compiler_params=pltpu.CompilerParams(
            collective_id=0, has_side_effects=True, vmem_limit_bytes=60 * 1024 * 1024
        ),
        name="nested_steps",
    )(
        adjoint,
        sea_mask,
        diffusivity,
        aggregation,
        breakup,
        sponge,
        settling,
        *(t.transpose(0, 2, 1) for t in tables),
    ).reshape(1, NCLS * LEV, CR, CC)


def solution(mesh):
    tile = P("grid", "gx", "gy")
    in_specs = (P("grid", None, "gx", "gy"),) + (tile,) * 5 + (P(),) * 4
    return jax.shard_map(
        local, mesh=mesh, in_specs=in_specs, out_specs=P("grid", None, "gx", "gy"), check_vma=False
    )
```

time: 80.2 us -> 71.6 us (0.89)
  Pallas kernels: 73.7 us -> 69.3 us
  local copies, waits for them, and re-layouts: 5.91 us -> 2.09 us
    pallas_call x1, Pallas kernels: 73.7 us -> 69.3 us  [local(): pl.pallas_call(kernel, out_shape=jax.ShapeDtypeStruct((1, NCLS, LEV, CR,...]
    unnamed x18 -> x1, local copies, waits for them, and re-layouts: 5.91 us -> 2.09 us
where the time goes in v2:
time: 71.6 us; the launch traced here: 71.4 us
  Pallas kernels  69.3 us (97%)
  local copies, waits for them, and re-layouts  2.09 us (3%)
    pallas_call x1, Pallas kernels, local(): pl.pallas_call(kernel, out_shape=jax.ShapeDtypeStruct((1, NCLS, LEV, CR,...  69.3 us
    unnamed x1, local copies, waits for them, and re-layouts  2.09 us

profile of v2, /device:TPU:1, one launch (start us, length us, event | category | flops | bytes accessed | tf_op | source)
XLA Modules:
  0.0 71.4 jit_solution(1022731929942806308)
XLA Ops:
  0.0 69.3 %nested_steps.1 = f32[1,3,8,32,256]{4,3,2,1,0:T(8,128)} custom-call(f32[1,24,32,256]{3,2,1,0:T(8,128)} %adjoint.1, s32[1,32,256]{2,1,0:T(8,128)} %sea_mask_in.1, f32[1,32,256]{2,1,0:T(8,128)} %diffusivity_in.1, f32[1,32,256]{2,1,0:T(8,128)} %aggregation_in.1, f32[1,32,256]{2,1,0:T(8,128)} %breakup_in.1, f32[1,32,256]{2,1,0:T(8,128)} %sponge_in.1, ...), custom_call_target="tpu_custom_call" | custom-call | tf_op jit(solution)/shard_map/nested_steps/pallas_call | solution.py:523
  69.3 2.1 %copy.12 = f32[1,24,32,256]{3,2,1,0:T(8,128)} copy(f32[1,24,32,256]{3,2,1,0:T(8,128)} %bitcast.4) | data formatting | bytes 1572864

commit v3 on v2

--- a/solution.py
+++ b/solution.py
@@ -30,7 +30,9 @@
 
 NORTH, SOUTH, WEST, EAST, UP, UP_X, RELAY, DOWN_X, DOWN = 0, 1, 2, 3, 4, 7, 8, 9, 10
 KINDS = 11
-LAG = 3
+SHORT, SHORT_END = 2, 8
+SHORTS = SHORT * (SHORT_END // CHUNKS)
+LAG = 2
 LEAD_SEND, LEAD_ANSWER, LEAD_RELAY = CHUNKS - LAG, 2, 4
 
 
@@ -217,6 +219,14 @@
             down_cross_send.at[trip], relayed.at[trip], RELAY, trip, {"grid": SLOTS, "gx": partner, "gy": behind}
         )
 
+    def short(trip):
+        return (lax.rem(trip, CHUNKS) < SHORT) & (trip < SHORT_END)
+
+    def direct_copy(trip):
+        return copy(
+            down_cross_send.at[trip], down_cross_recv.at[trip], RELAY, trip, {"gx": partner}, DOWN_X
+        )
+
     def down_cross_copy(trip):
         return copy(relayed.at[trip], down_cross_recv.at[trip], DOWN_X, trip, {"grid": 0, "gy": ahead})
 
@@ -283,7 +293,13 @@
                         base + level, c, tops[SLOTS + slot], lefts[SLOTS + slot]
                     )
 
-        relay_copy(trip).start()
+        @pl.when(short(trip))
+        def _():
+            direct_copy(trip).start()
+
+        @pl.when(jnp.logical_not(short(trip)))
+        def _():
+            relay_copy(trip).start()
 
     def send_down(trip, chunk):
         base = base_level(chunk)
@@ -450,31 +466,9 @@
     def _(tick):
         now = tick - LEAD_SEND
 
-        @pl.when(now >= LAG)
-        def _():
-            stencil(now - LAG, lax.rem(now - LAG + CHUNKS, CHUNKS))
-
-        @pl.when(now >= CHUNKS + LAG)
-        def _():
-            for store in stores(now - LAG - CHUNKS):
-                store.start()
-
-        sending = now + LEAD_SEND
-
-        @pl.when(sending < TRIPS)
-        def _():
-            first_sends(sending, lax.rem(sending, CHUNKS))
-
-        answering = now + LEAD_ANSWER
-
-        @pl.when(is_parent & in_range(answering))
-        def _():
-            send_down(answering, lax.rem(answering + CHUNKS, CHUNKS))
-            forward_up(answering)
-
         relaying = now + LEAD_RELAY
 
-        @pl.when(is_relay & in_range(relaying))
+        @pl.when(is_relay & in_range(relaying) & jnp.logical_not(short(relaying)))
         def _():
             relay(relaying)
 
@@ -491,6 +485,28 @@
                 nest_child(now, chunk)
 
             local_part(now, chunk)
+
+        @pl.when(now >= LAG)
+        def _():
+            stencil(now - LAG, lax.rem(now - LAG + CHUNKS, CHUNKS))
+
+        @pl.when(now >= CHUNKS + LAG)
+        def _():
+            for store in stores(now - LAG - CHUNKS):
+                store.start()
+
+        sending = now + LEAD_SEND
+
+        @pl.when(sending < TRIPS)
+        def _():
+            first_sends(sending, lax.rem(sending, CHUNKS))
+
+        answering = now + LEAD_ANSWER
+
+        @pl.when(is_parent & in_range(answering))
+        def _():
+            send_down(answering, lax.rem(answering + CHUNKS, CHUNKS))
+            forward_up(answering)
 
     def sent(source, kind, device):
         copy(source, source, kind, 0, device).wait_send()
@@ -510,7 +526,7 @@
 
     @pl.when(is_relay)
     def _():
-        sent(relayed, DOWN_X, {"grid": 0})
+        sent(relayed.at[pl.ds(0, TRIPS - SHORTS)], DOWN_X, {"grid": 0})
 
     @pl.loop(0, CHUNKS)
     def _(chunk):

time: 71.6 us -> 68.4 us (0.955)
  Pallas kernels: 69.3 us -> 66.1 us
    pallas_call x1, Pallas kernels: 69.3 us -> 66.1 us  [local(): pl.pallas_call(kernel, out_shape=jax.ShapeDtypeStruct((1, NCLS, LEV, CR,...]
where the time goes in v3:
time: 68.4 us; the launch traced here: 68.2 us
  Pallas kernels  66.1 us (97%)
  local copies, waits for them, and re-layouts  2.09 us (3%)
    pallas_call x1, Pallas kernels, local(): pl.pallas_call(kernel, out_shape=jax.ShapeDtypeStruct((1, NCLS, LEV, CR,...  66.1 us
    unnamed x1, local copies, waits for them, and re-layouts  2.09 us

profile of v3, /device:TPU:1, one launch (start us, length us, event | category | flops | bytes accessed | tf_op | source)
XLA Modules:
  0.0 68.2 jit_solution(17400066728208502694)
XLA Ops:
  0.0 66.1 %nested_steps.1 = f32[1,3,8,32,256]{4,3,2,1,0:T(8,128)} custom-call(f32[1,24,32,256]{3,2,1,0:T(8,128)} %adjoint.1, s32[1,32,256]{2,1,0:T(8,128)} %sea_mask_in.1, f32[1,32,256]{2,1,0:T(8,128)} %diffusivity_in.1, f32[1,32,256]{2,1,0:T(8,128)} %aggregation_in.1, f32[1,32,256]{2,1,0:T(8,128)} %breakup_in.1, f32[1,32,256]{2,1,0:T(8,128)} %sponge_in.1, ...), custom_call_target="tpu_custom_call" | custom-call | tf_op jit(solution)/shard_map/nested_steps/pallas_call | solution.py:539
  66.1 2.1 %copy.12 = f32[1,24,32,256]{3,2,1,0:T(8,128)} copy(f32[1,24,32,256]{3,2,1,0:T(8,128)} %bitcast.4) | data formatting | bytes 1572864

commit v4 on v3

--- a/solution.py
+++ b/solution.py
@@ -30,7 +30,8 @@
 
 NORTH, SOUTH, WEST, EAST, UP, UP_X, RELAY, DOWN_X, DOWN = 0, 1, 2, 3, 4, 7, 8, 9, 10
 KINDS = 11
-SHORT, SHORT_END = 2, 8
+LEAD_FORWARD = 3
+SHORT, SHORT_END = 3, 8
 SHORTS = SHORT * (SHORT_END // CHUNKS)
 LAG = 2
 LEAD_SEND, LEAD_ANSWER, LEAD_RELAY = CHUNKS - LAG, 2, 4
@@ -501,12 +502,17 @@
         def _():
             first_sends(sending, lax.rem(sending, CHUNKS))
 
+        forwarding = now + LEAD_FORWARD
+
+        @pl.when(is_parent & in_range(forwarding))
+        def _():
+            forward_up(forwarding)
+
         answering = now + LEAD_ANSWER
 
         @pl.when(is_parent & in_range(answering))
         def _():
             send_down(answering, lax.rem(answering + CHUNKS, CHUNKS))
-            forward_up(answering)
 
     def sent(source, kind, device):
         copy(source, source, kind, 0, device).wait_send()

time: 68.4 us -> 66.4 us (0.971)
  Pallas kernels: 66.1 us -> 64 us
    pallas_call x1, Pallas kernels: 66.1 us -> 64 us  [local(): pl.pallas_call(kernel, out_shape=jax.ShapeDtypeStruct((1, NCLS, LEV, CR,...]
where the time goes in v4:
time: 66.4 us; the launch traced here: 66.1 us
  Pallas kernels  64 us (96%)
  local copies, waits for them, and re-layouts  2.09 us (3%)
    pallas_call x1, Pallas kernels, local(): pl.pallas_call(kernel, out_shape=jax.ShapeDtypeStruct((1, NCLS, LEV, CR,...  64 us
    unnamed x1, local copies, waits for them, and re-layouts  2.09 us

profile of v4, /device:TPU:1, one launch (start us, length us, event | category | flops | bytes accessed | tf_op | source)
XLA Modules:
  0.0 66.1 jit_solution(18050494165579320612)
XLA Ops:
  0.0 64.0 %nested_steps.1 = f32[1,3,8,32,256]{4,3,2,1,0:T(8,128)} custom-call(f32[1,24,32,256]{3,2,1,0:T(8,128)} %adjoint.1, s32[1,32,256]{2,1,0:T(8,128)} %sea_mask_in.1, f32[1,32,256]{2,1,0:T(8,128)} %diffusivity_in.1, f32[1,32,256]{2,1,0:T(8,128)} %aggregation_in.1, f32[1,32,256]{2,1,0:T(8,128)} %breakup_in.1, f32[1,32,256]{2,1,0:T(8,128)} %sponge_in.1, ...), custom_call_target="tpu_custom_call" | custom-call | tf_op jit(solution)/shard_map/nested_steps/pallas_call | solution.py:545
  64.0 2.1 %copy.12 = f32[1,24,32,256]{3,2,1,0:T(8,128)} copy(f32[1,24,32,256]{3,2,1,0:T(8,128)} %bitcast.4) | data formatting | bytes 1572864

commit v5 on v4

--- a/solution.py
+++ b/solution.py
@@ -30,7 +30,7 @@
 
 NORTH, SOUTH, WEST, EAST, UP, UP_X, RELAY, DOWN_X, DOWN = 0, 1, 2, 3, 4, 7, 8, 9, 10
 KINDS = 11
-LEAD_FORWARD = 3
+LEAD_FORWARD = 4
 SHORT, SHORT_END = 3, 8
 SHORTS = SHORT * (SHORT_END // CHUNKS)
 LAG = 2

time: 66.4 us -> 69.1 us (1.041)
  Pallas kernels: 64 us -> 66.8 us
    pallas_call x1, Pallas kernels: 64 us -> 66.8 us  [local(): pl.pallas_call(kernel, out_shape=jax.ShapeDtypeStruct((1, NCLS, LEV, CR,...]
where the time goes in v5:
time: 69.1 us; the launch traced here: 68.9 us
  Pallas kernels  66.8 us (97%)
  local copies, waits for them, and re-layouts  2.09 us (3%)
    pallas_call x1, Pallas kernels, local(): pl.pallas_call(kernel, out_shape=jax.ShapeDtypeStruct((1, NCLS, LEV, CR,...  66.8 us
    unnamed x1, local copies, waits for them, and re-layouts  2.09 us

profile of v5, /device:TPU:1, one launch (start us, length us, event | category | flops | bytes accessed | tf_op | source)
XLA Modules:
  0.0 68.9 jit_solution(18372276992745628677)
XLA Ops:
  0.0 66.8 %nested_steps.1 = f32[1,3,8,32,256]{4,3,2,1,0:T(8,128)} custom-call(f32[1,24,32,256]{3,2,1,0:T(8,128)} %adjoint.1, s32[1,32,256]{2,1,0:T(8,128)} %sea_mask_in.1, f32[1,32,256]{2,1,0:T(8,128)} %diffusivity_in.1, f32[1,32,256]{2,1,0:T(8,128)} %aggregation_in.1, f32[1,32,256]{2,1,0:T(8,128)} %breakup_in.1, f32[1,32,256]{2,1,0:T(8,128)} %sponge_in.1, ...), custom_call_target="tpu_custom_call" | custom-call | tf_op jit(solution)/shard_map/nested_steps/pallas_call | solution.py:545
  66.8 2.1 %copy.12 = f32[1,24,32,256]{3,2,1,0:T(8,128)} copy(f32[1,24,32,256]{3,2,1,0:T(8,128)} %bitcast.4) | data formatting | bytes 1572864
